TPU v7x, 256 devices: a whole 4x4x8 slice. The times are simulated.
256 devices in a mesh: section: 8 (over z_hi, x), seq: 32 (over y, z_lo, core).
Axes of the slice: x: 4, y: 4, z: 8 (z_hi: 2, z_lo: 4; z = z_hi * 4 + z_lo), core: 2. Of those that a mesh axis runs over, the one named last changes fastest.
Arguments:
- input_keys: bfloat16 [8, 16384, 2048], P('section', 'seq'), may hold values from -6 to 6
- input_values: bfloat16 [8, 16384, 2048], P('section', 'seq'), may hold values from -6 to 6
- latent_queries: bfloat16 [8, 1024, 2048], P('section', 'seq'), may hold values from -6 to 6
- forward_out: bfloat16 [8, 1024, 2048], P('section', 'seq'), may hold values from -0.59765625 to 0.59765625
- log_norms: float32 [8, 1024, 16], P('section'), as said below
- block_table: int32 [8, 8], P('section'), may hold values from 0 to 127, as said below
- layer_grads: float32 [8, 8, 1024, 2048], P('section', None, 'seq'), may hold values from -600 to 600
Outputs:
- grad_keys: bfloat16 [8, 16384, 2048], P('section', 'seq')
- grad_values: bfloat16 [8, 16384, 2048], P('section', 'seq')
- grad_queries: bfloat16 [8, 1024, 2048], P('section', 'seq')
Inputs may be any that keep to these rules, and one draw needn't show every extreme that they name: block_table[b, a] is the last block of 128 input positions that latent block a sees; it rises strictly with a, it lies from 16 * (a + 1) - 8 to 16 * (a + 1) - 1, and the last latent block sees every position. log_norms[b, i, h] stand in for the saved normalizers: they are drawn near the log of the number of positions that latent i sees, plus 0.5, with noise of at most 0.45 either way.
All inputs are finite; a program needn't handle non-finite values.
Results may differ from a plain program's by a relative error of at most 0.0058.
Values may be sent and summed in bfloat16 or wider, within the bound.
No kernel may reach another device: no remote copies, remote signals or barrier semaphores. Data moves between devices by JAX's collectives and lax.ppermute only.
A program may use at most 128 MiB of HBM per device.

v0:
```python
import math
import jax
import jax.numpy as jnp
from jax import lax
from jax.sharding import PartitionSpec as P

BLK = 128


def body(
    input_keys, input_values, latent_queries, forward_out, log_norms, block_table, layer_grads
):
    arrived = lax.psum_scatter(layer_grads, "section", scatter_dimension=1, tiled=True)
    out_grad = arrived[0, 0].astype(jnp.bfloat16)
    head_count = log_norms.shape[2]
    width = input_keys.shape[2]
    head_dim = width // head_count
    score_scale = 1.0 / math.sqrt(head_dim)
    tok_count = input_keys.shape[1]
    limits = jnp.repeat(block_table[0], BLK)
    unit = lax.axis_index("seq")
    key_block = (unit * tok_count + jnp.arange(tok_count)) // BLK
    key_heads = input_keys[0].reshape(tok_count, head_count, head_dim).transpose(1, 0, 2)
    val_heads = input_values[0].reshape(tok_count, head_count, head_dim).transpose(1, 0, 2)
    lat_stack = jnp.stack([latent_queries[0], out_grad, forward_out[0]])
    all_lse = log_norms[0]
    lat_total = all_lse.shape[0]
    zeros_tok = jnp.zeros((head_count, tok_count, head_dim), jnp.float32)
    zeros_lat = jnp.zeros((lat_total, head_count, head_dim), jnp.float32)
    totals = (zeros_tok, zeros_tok, zeros_lat)
    latent_piece = lax.all_gather(lat_stack, "seq", axis=1, tiled=True)
    row_count = latent_piece.shape[1]
    step_rows = math.gcd(row_count, 256)
    step_count = row_count // step_rows
    split = latent_piece.reshape(3, step_count, step_rows, head_count, head_dim).transpose(
        1, 0, 2, 3, 4
    )

    def row_step(carry, inputs):
        key_total, value_total, query_total = carry
        lat_block, step_index = inputs
        row_start = step_index * step_rows
        queries = lat_block[0]
        grads = lat_block[1]
        lse_rows = lax.dynamic_slice_in_dim(all_lse, row_start, step_rows, 0)
        lim_rows = lax.dynamic_slice_in_dim(limits, row_start, step_rows, 0)
        visible = key_block[None, :] <= lim_rows[:, None]
        delta = jnp.sum(grads.astype(jnp.float32) * lat_block[2].astype(jnp.float32), axis=2)
        scores = (
            jnp.einsum("ihc,hjc->hij", queries, key_heads, preferred_element_type=jnp.float32)
            * score_scale
        )
        probs = jnp.where(visible[None], jnp.exp(scores - lse_rows.T[:, :, None]), 0.0)
        probs_low = probs.astype(jnp.bfloat16)
        dprobs = jnp.einsum("ihc,hjc->hij", grads, val_heads, preferred_element_type=jnp.float32)
        dscores = (probs * (dprobs - delta.T[:, :, None])).astype(jnp.bfloat16)
        query_part = jnp.einsum(
            "hij,hjc->ihc", dscores, key_heads, preferred_element_type=jnp.float32
        )
        key_total = key_total + jnp.einsum(
            "hij,ihc->hjc", dscores, queries, preferred_element_type=jnp.float32
        )
        value_total = value_total + jnp.einsum(
            "hij,ihc->hjc", probs_low, grads, preferred_element_type=jnp.float32
        )
        old_rows = lax.dynamic_slice_in_dim(query_total, row_start, step_rows, 0)
        query_total = lax.dynamic_update_slice_in_dim(
            query_total, old_rows + query_part, row_start, 0
        )
        return ((key_total, value_total, query_total), None)

    totals, ignored = lax.scan(row_step, totals, (split, jnp.arange(step_count, dtype=jnp.int32)))
    key_total, value_total, query_total = totals
    grad_k = (
        (key_total * score_scale).astype(jnp.bfloat16).transpose(1, 0, 2).reshape(tok_count, width)
    )
    grad_v = value_total.astype(jnp.bfloat16).transpose(1, 0, 2).reshape(tok_count, width)
    query_rows = lax.psum_scatter(
        query_total.reshape(lat_total, width) * score_scale, "seq", scatter_dimension=0, tiled=True
    )
    grad_q = query_rows.astype(jnp.bfloat16)
    return (grad_k[None], grad_v[None], grad_q[None])


def solution(mesh):
    placed = (
        P("section", "seq", None),
        P("section", "seq", None),
        P("section", "seq", None),
        P("section", "seq", None),
        P("section", None, None),
        P("section", None),
        P("section", None, "seq", None),
    )
    return jax.shard_map(
        body,
        mesh=mesh,
        in_specs=placed,
        out_specs=(P("section", "seq", None), P("section", "seq", None), P("section", "seq", None)),
        check_vma=False,
    )
```

profile of v0, /device:TPU:2, one launch (start us, length us, event | category | flops | bytes accessed | tf_op | source)
XLA Modules:
  0.0 489.3 jit_solution(8766786200359334464)
XLA Ops:
  8.0 102.2 %reduce-scatter.3.cloned.1.call-done = f32[1,1,32,2048]{3,2,1,0:T(8,128)} async-done(((f32[1,8,32,2048]{3,2,1,0:T(8,128)}), f32[1,1,32,2048]{3,2,1,0:T(8,128)}) %reduce-scatter.3.cloned.1.call-update) | async-done | bytes 262160 | tf_op jit(solution)/shard_map/reduce_scatter | solution.py:13
  118.6 4.0 copy.18
  122.5 3.9 copy.21
  126.5 61.8 %all-gather.2.cloned.1.call-done = bf16[3,1024,2048]{2,1,0:T(8,128)(2,1)} async-done(((bf16[3,32,2048]{2,1,0:T(8,128)(2,1)}), bf16[3,1024,2048]{2,1,0:T(8,128)(2,1)}) %all-gather.2.cloned.1.call-update) | async-done | bytes 12582928 | tf_op jit(solution)/shard_map/all_gather | solution.py:31
  188.3 11.4 %copy.32 = bf16[384,8,16,128]{3,2,1,0:T(8,128)(2,1)} copy(bf16[384,8,16,128]{3,1,2,0:T(8,128)(2,1)} %bitcast.89) | data formatting | bytes 25165824
  199.8 4.1 broadcast_in_dim.30
  203.8 106.4 %while.15 = (s32[]{:T(128)}, f32[16,512,128]{2,1,0:T(8,128)}, f32[16,512,128]{2,1,0:T(8,128)}, f32[1024,16,128]{2,0,1:T(8,128)}, s32[4]{0:T(128)S(1)}, /*index=5...) while((s32[]{:T(128)}, f32[16,512,128]{2,1,0:T(8,128)}, ...), condition=%wide.region_3.4_spmd.clone, body=%wide.region_1.3_spmd.clone.sunk | while | flops 2712276992 | bytes 86482224 | solution.py:72
  210.8 3.8 multiply_convert_fusion.3
  214.6 5.0 %select_add_fusion.5 = f32[16,512,128]{2,1,0:T(8,128)} fusion(f32[16,512,128]{2,1,0:T(8,128)} %get-tuple-element.234, pred[]{:T(512)S(6)} %compare.5, f32[16,256,512]{2,1,0:T(8,128)S(1)} %fusion.40, f32[16,256]{1,0:T(8,128)S(1)} %dynamic-slice_bitcast_fusion.2, pred[256,512]{1,0:T(8,128)(4,1)S(1)} %broadcast_compare_fusion.2, ...), kind=kOutput, calls=%fused_computation.5.clone.1 | convolution fusion | flops 547356672 | bytes 17973248 | tf_op jit(solution)/shard_map/while/body/eval_jaxpr/hij,ihc->hjc/dot_general | solution.py:63
  223.3 4.3 fusion.42
  234.7 3.8 multiply_convert_fusion.3
  238.5 6.6 %select_add_fusion.5 = f32[16,512,128]{2,1,0:T(8,128)} fusion(f32[16,512,128]{2,1,0:T(8,128)} %get-tuple-element.234, pred[]{:T(512)S(6)} %compare.5, f32[16,256,512]{2,1,0:T(8,128)S(1)} %fusion.40, f32[16,256]{1,0:T(8,128)S(1)} %dynamic-slice_bitcast_fusion.2, pred[256,512]{1,0:T(8,128)(4,1)S(1)} %broadcast_compare_fusion.2, ...), kind=kOutput, calls=%fused_computation.5.clone.1 | convolution fusion | flops 547356672 | bytes 17973248 | tf_op jit(solution)/shard_map/while/body/eval_jaxpr/hij,ihc->hjc/dot_general | solution.py:63
  245.0 5.8 %select_add_fusion.4 = f32[16,512,128]{2,1,0:T(8,128)} fusion(f32[16,512,128]{2,1,0:T(8,128)} %get-tuple-element.233, bf16[16,256,512]{2,1,0:T(8,128)(2,1)S(1)} %multiply_convert_fusion.3, pred[]{:T(512)S(6)} %compare.5, bf16[1,1,256,16,128]{4,3,2,0,1:T(8,128)(2,1)S(1)} %get-tuple-element.212), kind=kOutput, calls=%fused_computation.6.clone.1 | convolution fusion | flops 538968064 | bytes 13631489 | tf_op jit(solution)/shard_map/while/body/eval_jaxpr/hij,ihc->hjc/dot_general | solution.py:60
  250.9 4.3 fusion.42
  265.9 6.6 %select_add_fusion.5 = f32[16,512,128]{2,1,0:T(8,128)} fusion(f32[16,512,128]{2,1,0:T(8,128)} %get-tuple-element.234, pred[]{:T(512)S(6)} %compare.5, f32[16,256,512]{2,1,0:T(8,128)S(1)} %fusion.40, f32[16,256]{1,0:T(8,128)S(1)} %dynamic-slice_bitcast_fusion.2, pred[256,512]{1,0:T(8,128)(4,1)S(1)} %broadcast_compare_fusion.2, ...), kind=kOutput, calls=%fused_computation.5.clone.1 | convolution fusion | flops 547356672 | bytes 17973248 | tf_op jit(solution)/shard_map/while/body/eval_jaxpr/hij,ihc->hjc/dot_general | solution.py:63
  272.5 5.8 %select_add_fusion.4 = f32[16,512,128]{2,1,0:T(8,128)} fusion(f32[16,512,128]{2,1,0:T(8,128)} %get-tuple-element.233, bf16[16,256,512]{2,1,0:T(8,128)(2,1)S(1)} %multiply_convert_fusion.3, pred[]{:T(512)S(6)} %compare.5, bf16[1,1,256,16,128]{4,3,2,0,1:T(8,128)(2,1)S(1)} %get-tuple-element.212), kind=kOutput, calls=%fused_computation.6.clone.1 | convolution fusion | flops 538968064 | bytes 13631489 | tf_op jit(solution)/shard_map/while/body/eval_jaxpr/hij,ihc->hjc/dot_general | solution.py:60
  278.4 4.4 fusion.42
  289.8 3.8 multiply_convert_fusion.3
  293.6 6.6 %select_add_fusion.5 = f32[16,512,128]{2,1,0:T(8,128)} fusion(f32[16,512,128]{2,1,0:T(8,128)} %get-tuple-element.234, pred[]{:T(512)S(6)} %compare.5, f32[16,256,512]{2,1,0:T(8,128)S(1)} %fusion.40, f32[16,256]{1,0:T(8,128)S(1)} %dynamic-slice_bitcast_fusion.2, pred[256,512]{1,0:T(8,128)(4,1)S(1)} %broadcast_compare_fusion.2, ...), kind=kOutput, calls=%fused_computation.5.clone.1 | convolution fusion | flops 547356672 | bytes 17973248 | tf_op jit(solution)/shard_map/while/body/eval_jaxpr/hij,ihc->hjc/dot_general | solution.py:63
  300.1 5.8 %select_add_fusion.4 = f32[16,512,128]{2,1,0:T(8,128)} fusion(f32[16,512,128]{2,1,0:T(8,128)} %get-tuple-element.233, bf16[16,256,512]{2,1,0:T(8,128)(2,1)S(1)} %multiply_convert_fusion.3, pred[]{:T(512)S(6)} %compare.5, bf16[1,1,256,16,128]{4,3,2,0,1:T(8,128)(2,1)S(1)} %get-tuple-element.212), kind=kOutput, calls=%fused_computation.6.clone.1 | convolution fusion | flops 538968064 | bytes 13631489 | tf_op jit(solution)/shard_map/while/body/eval_jaxpr/hij,ihc->hjc/dot_general | solution.py:60
  306.0 4.3 fusion.42
  310.2 7.9 %copy_bitcast_fusion.7 = f32[1024,2048]{1,0:T(8,128)} fusion(f32[1024,16,128]{2,0,1:T(8,128)} %get-tuple-element.64), kind=kLoop, calls=%fused_computation.35 | loop fusion | flops 2097152 | bytes 16777216 | tf_op jit(solution)/shard_map/mul | solution.py:79
  318.1 5.9 %fusion.19 = (bf16[512,16,128]{2,0,1:T(8,128)(2,1)S(1)}, bf16[512,16,128]{2,0,1:T(8,128)(2,1)}) fusion(f32[16,512,128]{2,1,0:T(8,128)} %get-tuple-element.62, f32[16,512,128]{2,1,0:T(8,128)} %get-tuple-element.63), kind=kLoop, calls=%fused_computation.38 | loop fusion | flops 3145728 | bytes 12582912 | tf_op jit(solution)/shard_map/transpose | solution.py:75
  332.9 148.2 %reduce-scatter.5.cloned.1.call-done = f32[32,2048]{1,0:T(8,128)} async-done(((f32[1024,2048]{1,0:T(8,128)}), f32[32,2048]{1,0:T(8,128)}) %reduce-scatter.5.cloned.1.call-update) | async-done | bytes 262160 | tf_op jit(solution)/shard_map/reduce_scatter | solution.py:78
  (67 shorter events, 52.5 us)
Async XLA Ops:
  7.2 119.3 %copy-start = (s32[1,8]{1,0:T(1,128)S(1)}, s32[1,8]{1,0:T(1,128)}, u32[]{:S(2)}) copy-start(s32[1,8]{1,0:T(1,128)} %param.14) | copy-start | bytes 100
  7.2 105.9 %copy-start.2 = (bf16[1,512,2048]{2,1,0:T(8,128)(2,1)S(1)}, bf16[1,512,2048]{2,1,0:T(8,128)(2,1)}, u32[]{:S(2)}) copy-start(bf16[1,512,2048]{2,1,0:T(8,128)(2,1)} %param.9) | copy-start | bytes 6291460
  7.2 103.0 %reduce-scatter.3.cloned.1.call-start = ((), (), s32[]{:S(2)}) async-start(), calls=%async_computation.2 | async-start | bytes 2359296 | tf_op jit(solution)/shard_map/reduce_scatter | solution.py:13
  7.9 180.4 %all-gather.2.cloned.1.call-start = ((), (), s32[]{:S(2)}) async-start(), calls=%async_computation.3 | async-start | bytes 12976128 | tf_op jit(solution)/shard_map/all_gather | solution.py:31
  113.0 368.2 %reduce-scatter.5.cloned.1.call-start = ((), (), s32[]{:S(2)}) async-start(), calls=%async_computation.4 | async-start | bytes 8650752 | tf_op jit(solution)/shard_map/reduce_scatter | solution.py:78
  209.2 1.6 copy-start.3
  233.1 1.6 copy-start.3
  260.6 1.6 copy-start.3
  288.2 1.6 copy-start.3
  327.7 155.1 %copy-start.1 = (s32[1,8]{1,0:T(1,128)S(1)}, s32[1,8]{1,0:T(1,128)}, u32[]{:S(2)}) copy-start(s32[1,8]{1,0:T(1,128)} %param.14) | copy-start | bytes 100
Sparse Core Ops, SparseCore 0:
  12.1 98.0 reduce-scatter.2
  113.1 75.1 all-gather.1
  318.3 162.8 reduce-scatter.4
where the time goes:
time: 490 us; the launch traced here: 489 us
  waiting for transfers between devices  313 us (64%)
  matrix products  83.4 us (17%)
  local copies, waits for them, and re-layouts  54.4 us (11%)
  other arithmetic  22 us (4%)
  between operations  13.8 us (3%)
    reduce_scatter x1, waiting for transfers between devices, body(): lax.psum_scatter(query_total.reshape(lat_total, width) * score_scale, 'se...  148 us
    reduce_scatter x1, waiting for transfers between devices, body(): lax.psum_scatter(layer_grads, 'section', scatter_dimension=1, tiled=True)  102 us
    all_gather x1, waiting for transfers between devices, body(): latent_piece = lax.all_gather(lat_stack, 'seq', axis=1, tiled=True)  61.8 us
    unnamed x11, local copies, waits for them, and re-layouts  24.8 us
    dot_general x4, matrix products, row_step(): jnp.einsum('hij,ihc->hjc', probs_low, grads, preferred_element_type=jnp.f...  24.8 us
    dot_general x4, matrix products, row_step(): jnp.einsum('hij,ihc->hjc', dscores, queries, preferred_element_type=jnp.f...  21.2 us
    dot_general x4, matrix products, row_step(): jnp.einsum('hij,hjc->ihc', dscores, key_heads, preferred_element_type=jnp...  17.3 us
    dot_general x4, matrix products, row_step(): jnp.einsum('ihc,hjc->hij', grads, val_heads, preferred_element_type=jnp.f...  15.1 us
  transfers between devices with their start and end apart: 3, of which 3 were waited for; matrix products, arithmetic and copies ran while one was open for 6% of the time, Pallas kernels for 0%

commit v1 on v0

--- a/solution.py
+++ b/solution.py
@@ -28,7 +28,9 @@
     zeros_tok = jnp.zeros((head_count, tok_count, head_dim), jnp.float32)
     zeros_lat = jnp.zeros((lat_total, head_count, head_dim), jnp.float32)
     totals = (zeros_tok, zeros_tok, zeros_lat)
-    latent_piece = lax.all_gather(lat_stack, "seq", axis=1, tiled=True)
+    latent_piece = jnp.concatenate(
+        lax.all_to_all(jnp.stack([lat_stack] * lax.axis_size("seq")), "seq", 0, 0), axis=1
+    )
     row_count = latent_piece.shape[1]
     step_rows = math.gcd(row_count, 256)
     step_count = row_count // step_rows

time: 490 us -> 698 us (1.42)
  waiting for transfers between devices: 313 us -> 508 us
  local copies, waits for them, and re-layouts: 54.4 us -> 61.7 us
    all_to_all x0 -> x1, waiting for transfers between devices: none -> 262 us  [body(): lax.all_to_all(jnp.stack([lat_stack] * lax.axis_size('seq')), 'seq', 0, 0)]
    all_gather x1 -> x0, waiting for transfers between devices: 61.8 us -> none  [body(): latent_piece = lax.all_gather(lat_stack, 'seq', axis=1, tiled=True)]
  transfers between devices with their start and end apart: 3 -> 3, of which waited for: 3 -> 3; matrix products, arithmetic and copies ran while one was open for 6% -> 4% of each run, Pallas kernels for 0% -> 0%
where the time goes in v1:
time: 698 us; the launch traced here: 697 us
  waiting for transfers between devices  508 us (73%)
  matrix products  83.5 us (12%)
  local copies, waits for them, and re-layouts  61.7 us (9%)
  other arithmetic  21.2 us (3%)
  between operations  14.1 us (2%)
    all_to_all x1, waiting for transfers between devices, body(): lax.all_to_all(jnp.stack([lat_stack] * lax.axis_size('seq')), 'seq', 0, 0)  262 us
    reduce_scatter x1, waiting for transfers between devices, body(): lax.psum_scatter(query_total.reshape(lat_total, width) * score_scale, 'se...  144 us
    reduce_scatter x1, waiting for transfers between devices, body(): lax.psum_scatter(layer_grads, 'section', scatter_dimension=1, tiled=True)  102 us
    dot_general x4, matrix products, row_step(): jnp.einsum('hij,ihc->hjc', probs_low, grads, preferred_element_type=jnp.f...  24.8 us
    dot_general x4, matrix products, row_step(): jnp.einsum('hij,ihc->hjc', dscores, queries, preferred_element_type=jnp.f...  21.2 us
    unnamed x11, local copies, waits for them, and re-layouts  19.9 us
    dot_general x4, matrix products, row_step(): jnp.einsum('hij,hjc->ihc', dscores, key_heads, preferred_element_type=jnp...  17.3 us
    dot_general x4, matrix products, row_step(): jnp.einsum('ihc,hjc->hij', grads, val_heads, preferred_element_type=jnp.f...  15.1 us
  transfers between devices with their start and end apart: 3, of which 3 were waited for; matrix products, arithmetic and copies ran while one was open for 4% of the time, Pallas kernels for 0%

profile of v1, /device:TPU:2, one launch (start us, length us, event | category | flops | bytes accessed | tf_op | source)
XLA Modules:
  0.0 696.9 jit_solution(11496993914123666168)
XLA Ops:
  7.9 102.3 %reduce-scatter.3.cloned.1.call-done = f32[1,1,32,2048]{3,2,1,0:T(8,128)} async-done(((f32[1,8,32,2048]{3,2,1,0:T(8,128)}), f32[1,1,32,2048]{3,2,1,0:T(8,128)}) %reduce-scatter.3.cloned.1.call-update) | async-done | bytes 262160 | tf_op jit(solution)/shard_map/reduce_scatter | solution.py:13
  112.2 6.1 stack.5
  118.3 5.2 all-to-all-start
  129.1 3.9 copy.29
  133.0 3.9 copy.32
  137.0 261.6 %all-to-all-done = bf16[32,3,32,2048]{3,2,1,0:T(8,128)(2,1)} async-done(((bf16[32,3,32,2048]{3,2,1,0:T(8,128)(2,1)}), bf16[32,3,32,2048]{3,2,1,0:T(8,128)(2,1)}, u32[]{:S(2)}, u32[]{:S(2)}) %all-to-all-start) | async-done | bytes 12582944 | tf_op jit(solution)/shard_map/all_to_all | solution.py:32
  398.6 6.2 copy.27
  404.8 6.5 copy.43
  411.3 4.1 broadcast_in_dim.30
  415.4 106.5 %while.15 = (s32[]{:T(128)}, f32[16,512,128]{2,1,0:T(8,128)}, f32[16,512,128]{2,1,0:T(8,128)}, f32[1024,16,128]{2,0,1:T(8,128)}, s32[4]{0:T(128)S(1)}, /*index=5...) while((s32[]{:T(128)}, f32[16,512,128]{2,1,0:T(8,128)}, ...), condition=%wide.region_3.4_spmd.clone, body=%wide.region_1.3_spmd.clone.sunk | while | flops 2712276992 | bytes 86482224 | solution.py:74
  426.2 5.0 select_add_fusion.5
  434.9 4.3 fusion.42
  450.0 6.6 select_add_fusion.5
  456.6 5.8 select_add_fusion.4
  462.5 4.3 fusion.42
  477.6 6.6 select_add_fusion.5
  484.2 5.8 select_add_fusion.4
  490.0 4.4 fusion.42
  505.3 6.6 select_add_fusion.5
  511.9 5.8 select_add_fusion.4
  517.7 4.2 fusion.42
  521.9 7.8 %copy_bitcast_fusion.7 = f32[1024,2048]{1,0:T(8,128)} fusion(f32[1024,16,128]{2,0,1:T(8,128)} %get-tuple-element.64), kind=kLoop, calls=%fused_computation.35 | loop fusion | flops 2097152 | bytes 16777216 | tf_op jit(solution)/shard_map/mul | solution.py:81
  529.8 5.9 fusion.19
  544.6 143.8 %reduce-scatter.5.cloned.1.call-done = f32[32,2048]{1,0:T(8,128)} async-done(((f32[1024,2048]{1,0:T(8,128)}), f32[32,2048]{1,0:T(8,128)}) %reduce-scatter.5.cloned.1.call-update) | async-done | bytes 262160 | tf_op jit(solution)/shard_map/reduce_scatter | solution.py:80
  (68 shorter events, 63.2 us)
Async XLA Ops:
  7.2 129.8 %copy-start = (s32[1,8]{1,0:T(1,128)S(1)}, s32[1,8]{1,0:T(1,128)}, u32[]{:S(2)}) copy-start(s32[1,8]{1,0:T(1,128)} %param.14) | copy-start | bytes 100
  7.2 103.0 %reduce-scatter.3.cloned.1.call-start = ((), (), s32[]{:S(2)}) async-start(), calls=%async_computation.3 | async-start | bytes 2359296 | tf_op jit(solution)/shard_map/reduce_scatter | solution.py:13
  118.3 5.3 copy-start.2
  118.3 280.4 %all-to-all-start = ((bf16[32,3,32,2048]{3,2,1,0:T(8,128)(2,1)}), bf16[32,3,32,2048]{3,2,1,0:T(8,128)(2,1)}, u32[]{:S(2)}, u32[]{:S(2)}) async-start(bf16[32,3,32,2048]{3,2,1,0:T(8,128)(2,1)} %stack.5), calls=%async_computation.1 | async-start | bytes 25165824 | tf_op jit(solution)/shard_map/all_to_all | solution.py:32
  123.5 564.9 %reduce-scatter.5.cloned.1.call-start = ((), (), s32[]{:S(2)}) async-start(), calls=%async_computation.4 | async-start | bytes 8650752 | tf_op jit(solution)/shard_map/reduce_scatter | solution.py:80
  420.8 1.6 copy-start.3
  444.6 1.6 copy-start.3
  472.2 1.6 copy-start.3
  499.9 1.6 copy-start.3
  539.3 150.7 %copy-start.1 = (s32[1,8]{1,0:T(1,128)S(1)}, s32[1,8]{1,0:T(1,128)}, u32[]{:S(2)}) copy-start(s32[1,8]{1,0:T(1,128)} %param.14) | copy-start | bytes 100
Sparse Core Ops, SparseCore 0:
  12.1 98.0 reduce-scatter.2
  529.9 158.4 reduce-scatter.4
